TPU v7x, 1024 devices: a whole 4x4x32 slice. The times are simulated.
1024 devices in a mesh: section: 16 (over y, x_hi, core), fsdp: 32 (over z), tp: 2 (over x_lo).
Axes of the slice: x: 4 (x_hi: 2, x_lo: 2; x = x_hi * 2 + x_lo), y: 4, z: 32, core: 2. Of those that a mesh axis runs over, the one named last changes fastest.
Arguments:
- text_tokens: bfloat16 [65536, 8192], P(('section', 'fsdp')), may hold values from -45 to 45
- images: bfloat16 [256, 256, 8192], P('section', None, ('fsdp', 'tp')), may hold values from -45 to 45
- counts: int32 [256], P('section'), may hold values from 1 to 256, as said below
- offsets: int32 [256], P('section'), may hold values from 0 to 65535, as said below
- norm_gain: float32 [8192], replicated, may hold values from 0.25 to 1.75
- value_weight: bfloat16 [8192, 512], P(('fsdp', 'tp'), 'section'), may hold values from -0.0625 to 0.0625
- value_grad: bfloat16 [65536, 512], P(('section', 'fsdp')), may hold values from -6 to 6
Outputs:
- values: bfloat16 [65536, 512], P(('section', 'fsdp'), 'tp')
- visual_grads: bfloat16 [256, 256, 8192], P('section', None, ('fsdp', 'tp'))
Inputs may be any that keep to these rules, and one draw needn't show every extreme that they name: `counts`: on every section index some tile has exactly 256 visual tokens. Tile i occupies positions offsets[i] to offsets[i] + counts[i] - 1, all inside one aligned block of 256 positions. The positions of one section index form 16 such blocks. The 16 tiles of one section index go to 16 different section indices, and every block receives exactly one tile.
All inputs are finite; a program needn't handle non-finite values.
Results may differ from a plain program's by a relative error of at most 0.0049.
Values may be sent and summed in bfloat16 or wider, within the bound.
No kernel may reach another device: no remote copies, remote signals or barrier semaphores. Data moves between devices by JAX's collectives and lax.ppermute only.
A program may use at most 64 MiB of HBM per device.

v0:
```python
import jax
import jax.numpy as jnp
from jax import lax
from jax.sharding import PartitionSpec as P


epsilon = 1e-05


def swapped(x, axis, bit):
    length = lax.axis_size(axis)
    return lax.ppermute(x, axis, [(i, i ^ bit) for i in range(length)])


def joined(x, axis, bit):
    other = swapped(x, axis, bit)
    is_high = (lax.axis_index(axis) & bit) != 0
    return jnp.stack([jnp.where(is_high, other, x), jnp.where(is_high, x, other)])


def gathered_by_bits(x, axis):
    length = lax.axis_size(axis)
    rest = x.shape
    bits = length.bit_length() - 1
    for b in range(bits - 1, -1, -1):
        x = joined(x, axis, 1 << b)
    order = tuple(range(bits - 1, -1, -1))
    return x.transpose(order + tuple(range(bits, bits + len(rest)))).reshape(length, *rest)


def fetched(x, axis, distance):
    length = lax.axis_size(axis)
    return lax.ppermute(x, axis, [(i, (i - distance) % length) for i in range(length)])


def gathered_by_windows(x, axis):
    length = lax.axis_size(axis)
    strides = length // 8
    far = [x]
    for a in range(1, strides):
        far.append(fetched(x, axis, 8 * a))
    far = jnp.stack(far)
    ahead, ahead2, behind = (fetched(far, axis, d) for d in (2, 4, -2))
    behind = jnp.concatenate([behind[1:], behind[:1]])
    even = jnp.stack([behind, far, ahead, ahead2])
    above = fetched(even[1:3], axis, 1)
    below = fetched(even[0:2], axis, -1)
    last = jnp.concatenate([below[1, 1:], below[1, :1]])
    pieces = [far, above[0], ahead, above[1], ahead2, below[0], behind, last]
    relative = jnp.stack(pieces, axis=1).reshape(length, *x.shape)
    twice = jnp.concatenate([relative, relative])
    return lax.dynamic_slice_in_dim(twice, length - lax.axis_index(axis), length, 0)


def on_device(text_tokens, images, counts, offsets, norm_gain, value_weight, value_grad):
    sections = lax.axis_size("section")
    columns = lax.axis_size("fsdp")
    pair_count = lax.axis_size("tp")
    tok_rows, feature_width = text_tokens.shape
    img_count, most_slots, feature_slice = images.shape
    width = value_grad.shape[1]
    own_columns = value_weight.shape[1]
    half_width = width // pair_count
    half_rows = tok_rows // pair_count
    halves = most_slots // tok_rows
    group_rows = columns * tok_rows
    pair_index = lax.axis_index("tp")
    column_index = lax.axis_index("fsdp")
    is_second = pair_index == 1
    plane = ("section", "tp")
    w_rows_first = value_weight.T

    own_half = lax.dynamic_index_in_dim(
        value_grad.reshape(pair_count, half_rows, width), pair_index, 0, keepdims=False
    )
    own_half = lax.optimization_barrier(own_half)
    sent_rows = jnp.concatenate([own_half, w_rows_first.reshape(-1, width)])
    column_rows = gathered_by_windows(sent_rows, "fsdp")
    grads_in = column_rows[:, :half_rows]
    w_column = column_rows[:, half_rows:].reshape(columns, own_columns, feature_slice)

    target = offsets // group_rows
    within = offsets % group_rows
    region = within // most_slots
    first_slot = within % most_slots
    section_ids = jnp.arange(sections, dtype=jnp.int32)
    slot_ids = jnp.arange(most_slots, dtype=jnp.int32)
    is_valid = slot_ids[None, :] < counts[:, None]
    placing = (
        (slot_ids[None, :, None] == first_slot[:, None, None] + slot_ids[None, None, :])
        & is_valid[:, None, :]
    ).astype(jnp.bfloat16)
    routing = target[:, None] == section_ids[None, :]
    route_float = routing.astype(jnp.bfloat16)
    route_int = routing.astype(jnp.int32)
    meta_rows = jnp.stack([region, first_slot, counts], axis=1)
    meta_out = jnp.sum(route_int[:, :, None] * meta_rows[:, None, :], axis=0)
    meta_in = lax.all_to_all(meta_out, "section", split_axis=0, concat_axis=0, tiled=True)

    placed = jnp.einsum("krj,kjd->krd", placing, images, preferred_element_type=jnp.float32).astype(
        jnp.bfloat16
    )
    outgoing = jnp.einsum(
        "kt,krd->trd", route_float, placed, preferred_element_type=jnp.float32
    ).astype(jnp.bfloat16)
    outgoing = outgoing.reshape(sections, halves, pair_count, half_rows, feature_slice)
    outgoing = outgoing.transpose(0, 2, 1, 3, 4).reshape(-1, halves * half_rows, feature_slice)
    w_copies = jnp.broadcast_to(w_rows_first[None], (outgoing.shape[0], *w_rows_first.shape))
    arrived = lax.all_to_all(jnp.concatenate([outgoing, w_copies], axis=1), plane, 0, 0, tiled=True)
    arrived = arrived.reshape(sections, pair_count, -1, feature_slice)
    w_here = arrived[:, :, halves * half_rows :]
    order_int = (meta_in[:, 0:1] == section_ids[None, :]).astype(jnp.int32)
    order_float = order_int.astype(jnp.bfloat16)
    rows = jnp.einsum(
        "sr,stpd->trpd",
        order_float,
        arrived[:, :, : halves * half_rows],
        preferred_element_type=jnp.float32,
    ).astype(jnp.bfloat16)
    rows = rows.reshape(pair_count, columns * half_rows, feature_slice)
    w_here = w_here.transpose(1, 0, 2, 3).reshape(pair_count, width, feature_slice)
    gain_pairs = norm_gain.reshape(columns, pair_count, feature_slice)
    gain_here = lax.dynamic_index_in_dim(gain_pairs, column_index, 0, keepdims=False)
    w_here_gain = (w_here.astype(jnp.float32) * gain_here[:, None, :]).astype(jnp.bfloat16)

    part = sum(
        lax.dot_general(
            rows[t],
            w_here_gain[t],
            (((1,), (1,)), ((), ())),
            preferred_element_type=jnp.float32,
        )
        for t in range(pair_count)
    )
    rows_f = [rows[t].astype(jnp.float32) for t in range(pair_count)]
    squares = jnp.sum(sum(r * r for r in rows_f), axis=1, keepdims=True)
    part = jnp.concatenate([part, jnp.broadcast_to(squares, (squares.shape[0], 128))], axis=1)
    own_sums = lax.psum_scatter(part, "fsdp", scatter_dimension=0, tiled=True)
    image_raw = own_sums[:, :width]
    own_inv = lax.rsqrt(own_sums[:, width] / feature_width + epsilon)
    own_inner = jnp.sum(image_raw * own_half.astype(jnp.float32), axis=1)
    own_factor = own_inv * own_inv * own_inv * own_inner / feature_width

    scalars = jnp.stack([own_inv, own_factor]).reshape(1, 1, -1)
    scalars = lax.all_to_all(
        jnp.broadcast_to(scalars, (columns, 1, 2 * half_rows)), "fsdp", 0, 0, tiled=True
    )
    scalars = scalars.reshape(sections, -1)
    scalars = jnp.sum(order_int.astype(jnp.float32)[:, :, None] * scalars[None], axis=1)
    scalars = jnp.broadcast_to(scalars[:, None], (sections, pair_count, scalars.shape[1]))
    scalars = lax.all_to_all(scalars.reshape(sections * pair_count, 2, -1), plane, 0, 0, tiled=True)
    scalars = scalars.reshape(1, sections, -1)
    scalars = jnp.sum(routing.astype(jnp.float32)[:, :, None] * scalars, axis=1)
    scalars = scalars.reshape(img_count, pair_count, halves, 2, half_rows).transpose(0, 3, 2, 1, 4)
    scalars = scalars.reshape(img_count, 2, most_slots)

    grads_flat = grads_in.reshape(-1, width)
    by_source = []
    for t in range(pair_count):
        weighted = lax.dot_general(
            grads_flat, w_here[t], (((1,), (0,)), ((), ())), preferred_element_type=jnp.float32
        )
        weighted = (weighted * gain_here[t]).astype(jnp.bfloat16)
        weighted = weighted.reshape(sections, halves * half_rows, feature_slice)
        by_source.append(
            jnp.einsum("sr,rpd->spd", order_float, weighted, preferred_element_type=jnp.float32)
        )
    by_source = jnp.stack(by_source, axis=1).astype(jnp.bfloat16)
    returned = lax.all_to_all(
        by_source.reshape(-1, halves * half_rows, feature_slice), plane, 0, 0, tiled=True
    )
    returned = returned.reshape(sections, pair_count, halves, half_rows, feature_slice)
    returned = returned.transpose(0, 2, 1, 3, 4).reshape(sections, most_slots, feature_slice)
    own_weighted = jnp.einsum(
        "kt,trd->krd", route_float, returned, preferred_element_type=jnp.float32
    )
    grad_rows = (
        scalars[:, 0, :, None] * own_weighted
        - placed.astype(jnp.float32) * scalars[:, 1, :, None]
    ).astype(jnp.bfloat16)
    visual_grads = jnp.einsum(
        "krj,krd->kjd", placing, grad_rows, preferred_element_type=jnp.float32
    ).astype(jnp.bfloat16)

    w_all = gathered_by_bits(w_column.transpose(1, 0, 2), "section").reshape(width, -1)
    text_split = text_tokens.reshape(tok_rows, columns, pair_count, feature_slice)
    text_own = lax.dynamic_index_in_dim(text_split, pair_index, 2, keepdims=False)
    gain_own = lax.dynamic_index_in_dim(gain_pairs, pair_index, 1, keepdims=False)
    text_gain = (text_own.astype(jnp.float32) * gain_own[None]).astype(jnp.bfloat16)
    text_f = text_tokens.astype(jnp.float32)
    text_inv = lax.rsqrt(jnp.sum(text_f * text_f, axis=1, keepdims=True) / feature_width + epsilon)
    text_raw = lax.dot_general(
        text_gain.reshape(tok_rows, -1),
        w_all,
        (((1,), (1,)), ((), ())),
        preferred_element_type=jnp.float32,
    )
    text_kept = jnp.where(is_second, text_raw[:, half_width:], text_raw[:, :half_width])
    text_sent = jnp.where(is_second, text_raw[:, :half_width], text_raw[:, half_width:])
    text_got = swapped(text_sent, "tp", 1)
    text_values = ((text_kept + text_got) * text_inv).astype(jnp.bfloat16)

    image_values = (image_raw * own_inv[:, None]).astype(jnp.bfloat16)
    image_kept = jnp.where(is_second, image_values[:, half_width:], image_values[:, :half_width])
    image_sent = jnp.where(is_second, image_values[:, :half_width], image_values[:, half_width:])
    image_got = swapped(image_sent, "tp", 1)
    image_rows = jnp.concatenate(
        [
            jnp.where(is_second, image_got, image_kept),
            jnp.where(is_second, image_kept, image_got),
        ]
    )

    region_start = jnp.sum(order_int * meta_in[:, 1:2], axis=0)
    region_count = jnp.sum(order_int * meta_in[:, 2:3], axis=0)
    row_ids = column_index * tok_rows + jnp.arange(tok_rows, dtype=jnp.int32)
    row_region = ((row_ids // most_slots)[:, None] == section_ids[None, :]).astype(jnp.int32)
    row_local = row_ids % most_slots
    row_start = jnp.sum(row_region * region_start[None, :], axis=1)
    row_count = jnp.sum(row_region * region_count[None, :], axis=1)
    covered = (row_local >= row_start) & (row_local < row_start + row_count)
    values = jnp.where(covered[:, None], image_rows, text_values)
    return (values, visual_grads)


def solution(mesh):
    placed = (
        P(("section", "fsdp"), None),
        P("section", None, ("fsdp", "tp")),
        P("section"),
        P("section"),
        P(),
        P(("fsdp", "tp"), "section"),
        P(("section", "fsdp"), None),
    )

    return jax.shard_map(
        on_device,
        mesh=mesh,
        in_specs=placed,
        out_specs=(P(("section", "fsdp"), "tp"), P("section", None, ("fsdp", "tp"))),
        check_vma=False,
    )
```

profile of v0, /device:TPU:1, one launch (start us, length us, event | category | flops | bytes accessed | tf_op | source)
XLA Modules:
  0.0 384.9 jit_solution(12455920523487149453)
XLA Ops:
  10.1 17.4 %all-to-all-start = ((s32[16,1,3]{2,1,0:T(1,128)}), s32[16,1,3]{2,1,0:T(1,128)S(1)}, u32[]{:S(2)}, u32[]{:S(2)}) async-start(s32[16,1,3]{2,1,0:T(1,128)} %copy.115), calls=%async_computation | async-start | bytes 16384 | tf_op jit(solution)/shard_map/all_to_all | solution.py:98
  28.3 3.0 fusion.17
  34.5 6.7 %all-to-all-start.1 = ((bf16[32,160,128]{2,1,0:T(8,128)(2,1)}), bf16[32,160,128]{2,1,0:T(8,128)(2,1)S(1)}, u32[]{:S(2)}, u32[]{:S(2)}) async-start(bf16[32,160,128]{2,1,0:T(8,128)(2,1)} %pad_maximum_fusion.2), calls=%async_computation.1 | async-start | bytes 2621440 | tf_op jit(solution)/shard_map/all_to_all | solution.py:109
  42.0 17.2 %all-to-all-done.1 = bf16[32,160,128]{2,1,0:T(8,128)(2,1)S(1)} async-done(((bf16[32,160,128]{2,1,0:T(8,128)(2,1)}), bf16[32,160,128]{2,1,0:T(8,128)(2,1)S(1)}, u32[]{:S(2)}, u32[]{:S(2)}) %all-to-all-start.1) | async-done | bytes 1310752 | tf_op jit(solution)/shard_map/all_to_all | solution.py:109
  63.5 3.0 pad_maximum_fusion
  66.5 5.9 %copy.143 = f32[2048,640]{1,0:T(8,128)} copy(f32[2048,640]{0,1:T(8,128)} %pad_maximum_fusion) | data formatting | bytes 10485760
  73.4 13.7 %collective-permute-start.1 = (bf16[72,512]{1,0:T(8,128)(2,1)S(1)}, bf16[72,512]{1,0:T(8,128)(2,1)S(1)}, u32[]{:S(2)}, u32[]{:S(2)}) collective-permute-start(bf16[72,512]{1,0:T(8,128)(2,1)S(1)} %get-tuple-element.38), channel_id=1, source_target_pairs={{0,48},{2,50},{4,52},{6,54},{8,56},{10,58},{12,60},{14,62},{16,0},... | collective-permute-start | bytes 221192 | tf_op jit(solution)/shard_map/ppermute | solution.py:33
  87.1 7.9 %collective-permute-start.2 = (bf16[72,512]{1,0:T(8,128)(2,1)S(1)}, bf16[72,512]{1,0:T(8,128)(2,1)S(1)}, u32[]{:S(2)}, u32[]{:S(2)}) collective-permute-start(bf16[72,512]{1,0:T(8,128)(2,1)S(1)} %get-tuple-element.38), channel_id=1, source_target_pairs={{0,32},{2,34},{4,36},{6,38},{8,40},{10,42},{12,44},{14,46},{16,48}... | collective-permute-start | bytes 221192 | tf_op jit(solution)/shard_map/ppermute | solution.py:33
  95.0 12.1 %collective-permute-start.3 = (bf16[72,512]{1,0:T(8,128)(2,1)S(1)}, bf16[72,512]{1,0:T(8,128)(2,1)S(1)}, u32[]{:S(2)}, u32[]{:S(2)}) collective-permute-start(bf16[72,512]{1,0:T(8,128)(2,1)S(1)} %get-tuple-element.38), channel_id=1, source_target_pairs={{0,16},{2,18},{4,20},{6,22},{8,24},{10,26},{12,28},{14,30},{16,32}... | collective-permute-start | bytes 221192 | tf_op jit(solution)/shard_map/ppermute | solution.py:33
  107.1 4.1 %collective-permute-done.2 = bf16[72,512]{1,0:T(8,128)(2,1)S(1)} collective-permute-done((bf16[72,512]{1,0:T(8,128)(2,1)S(1)}, bf16[72,512]{1,0:T(8,128)(2,1)S(1)}, u32[]{:S(2)}, u32[]{:S(2)}) %collective-permute-start.2) | collective-permute-done | bytes 73760 | tf_op jit(solution)/shard_map/ppermute | solution.py:33
  111.2 13.2 %collective-permute-done.3 = bf16[72,512]{1,0:T(8,128)(2,1)S(1)} collective-permute-done((bf16[72,512]{1,0:T(8,128)(2,1)S(1)}, bf16[72,512]{1,0:T(8,128)(2,1)S(1)}, u32[]{:S(2)}, u32[]{:S(2)}) %collective-permute-start.3) | collective-permute-done | bytes 73760 | tf_op jit(solution)/shard_map/ppermute | solution.py:33
  126.4 5.5 %collective-permute-start.4 = (bf16[4,72,512]{2,1,0:T(8,128)(2,1)S(1)}, bf16[4,72,512]{2,1,0:T(8,128)(2,1)S(1)}, u32[]{:S(2)}, u32[]{:S(2)}) collective-permute-start(bf16[4,72,512]{2,1,0:T(8,128)(2,1)S(1)} %get-tuple-element.30), channel_id=1, source_target_pairs={{0,60},{2,62},{4,0},{6,2},{8,4},{10,6},{12,8},{14,10},{16,12},{18,... | collective-permute-start | bytes 884744 | tf_op jit(solution)/shard_map/ppermute | solution.py:33
  131.9 3.7 collective-permute-done.7
  136.7 15.8 %collective-permute-start.5 = (bf16[2,4,72,512]{3,2,1,0:T(8,128)(2,1)S(1)}, bf16[2,4,72,512]{3,2,1,0:T(8,128)(2,1)S(1)}, u32[]{:S(2)}, u32[]{:S(2)}) collective-permute-start(bf16[2,4,72,512]{3,2,1,0:T(8,128)(2,1)S(1)} %get-tuple-element.28), channel_id=1, source_target_pairs={{0,62},{2,0},{4,2},{6,4},{8,6},{10,8},{12,10},{14,12},{16,14},{18,... | collective-permute-start | bytes 1769480 | tf_op jit(solution)/shard_map/ppermute | solution.py:33
  152.5 5.4 %collective-permute-start.6 = (bf16[4,72,512]{2,1,0:T(8,128)(2,1)S(1)}, bf16[4,72,512]{2,1,0:T(8,128)(2,1)S(1)}, u32[]{:S(2)}, u32[]{:S(2)}) collective-permute-start(bf16[4,72,512]{2,1,0:T(8,128)(2,1)S(1)} %get-tuple-element.30), channel_id=1, source_target_pairs={{0,56},{2,58},{4,60},{6,62},{8,0},{10,2},{12,4},{14,6},{16,8},{18,... | collective-permute-start | bytes 884744 | tf_op jit(solution)/shard_map/ppermute | solution.py:33
  159.9 14.5 %collective-permute-done.5 = bf16[2,4,72,512]{3,2,1,0:T(8,128)(2,1)S(1)} collective-permute-done((bf16[2,4,72,512]{3,2,1,0:T(8,128)(2,1)S(1)}, bf16[2,4,72,512]{3,2,1,0:T(8,128)(2,1)S(1)}, u32[]{:S(2)}, u32[]{:S(2)}) %collective-permute-start.5) | collective-permute-done | bytes 589856 | tf_op jit(solution)/shard_map/ppermute | solution.py:33
  174.4 19.1 %collective-permute-done.6 = bf16[4,72,512]{2,1,0:T(8,128)(2,1)S(1)} collective-permute-done((bf16[4,72,512]{2,1,0:T(8,128)(2,1)S(1)}, bf16[4,72,512]{2,1,0:T(8,128)(2,1)S(1)}, u32[]{:S(2)}, u32[]{:S(2)}) %collective-permute-start.6) | collective-permute-done | bytes 294944 | tf_op jit(solution)/shard_map/ppermute | solution.py:33
  195.0 23.5 %collective-permute-start.9 = (bf16[32,32,128]{2,0,1:T(8,128)(2,1)S(1)}, bf16[32,32,128]{2,0,1:T(8,128)(2,1)S(1)}, u32[]{:S(2)}, u32[]{:S(2)}) collective-permute-start(bf16[32,32,128]{2,0,1:T(8,128)(2,1)S(1)} %bitcast.182), channel_id=1, source_target_pairs={{0,512},{64,576},{128,640},{192,704},{256,768},{320,832},{384,896}... | collective-permute-start | bytes 786440 | tf_op jit(solution)/shard_map/ppermute | solution.py:12
  218.5 3.7 collective-permute-done.9
  224.3 8.5 %collective-permute-done.10 = bf16[2,32,32,128]{3,1,2,0:T(8,128)(2,1)} collective-permute-done((bf16[2,32,32,128]{3,1,2,0:T(8,128)(2,1)S(1)}, bf16[2,32,32,128]{3,1,2,0:T(8,128)(2,1)}, u32[]{:S(2)}, u32[]{:S(2)}) %collective-permute-start.10) | collective-permute-done | bytes 524320 | tf_op jit(solution)/shard_map/ppermute | solution.py:12
  235.2 3.7 collective-permute-start.11
  239.5 4.1 %copy.128 = bf16[128,8192]{0,1:T(8,128)(2,1)} copy(bf16[128,8192]{1,0:T(8,128)(2,1)} %param.7) | data formatting | bytes 4194304 | tf_op args[0]
  246.8 11.0 %collective-permute-done.11 = bf16[2,2,32,32,128]{4,2,3,1,0:T(8,128)(2,1)} collective-permute-done((bf16[2,2,32,32,128]{4,2,3,1,0:T(8,128)(2,1)}, bf16[2,2,32,32,128]{4,2,3,1,0:T(8,128)(2,1)}, u32[]{:S(2)}, u32[]{:S(2)}) %collective-permute-start.11) | collective-permute-done | bytes 1048608 | tf_op jit(solution)/shard_map/ppermute | solution.py:12
  260.7 8.8 %collective-permute-start.12 = (bf16[2,2,2,32,32,128]{5,3,4,2,1,0:T(8,128)(2,1)}, bf16[2,2,2,32,32,128]{5,3,4,2,1,0:T(8,128)(2,1)}, u32[]{:S(2)}, u32[]{:S(2)}) collective-permute-start(bf16[2,2,2,32,32,128]{5,3,4,2,1,0:T(8,128)(2,1)} %pad_maximum_fusion.1), channel_id=1, source_target_pairs={{0,64},{64,0},{128,192},{192,128},{256,320},{320,256},{384,448},{4... | collective-permute-start | bytes 6291464 | tf_op jit(solution)/shard_map/ppermute | solution.py:12
  273.3 9.8 %all-to-all-start.4 = ((bf16[32,128,128]{2,1,0:T(8,128)(2,1)}), bf16[32,128,128]{2,1,0:T(8,128)(2,1)S(1)}, u32[]{:S(2)}, u32[]{:S(2)}) async-start(bf16[32,128,128]{2,1,0:T(8,128)(2,1)} %bitcast.173), calls=%async_computation.4 | async-start | bytes 2097152 | tf_op jit(solution)/shard_map/all_to_all | solution.py:169
  285.9 12.8 %all-to-all-done.4 = bf16[32,128,128]{2,1,0:T(8,128)(2,1)S(1)} async-done(((bf16[32,128,128]{2,1,0:T(8,128)(2,1)}), bf16[32,128,128]{2,1,0:T(8,128)(2,1)S(1)}, u32[]{:S(2)}, u32[]{:S(2)}) %all-to-all-start.4) | async-done | bytes 1048608 | tf_op jit(solution)/shard_map/all_to_all | solution.py:169
  311.4 3.4 collective-permute-start
  315.5 18.3 %all-to-all-start.2 = ((f32[32,1,128]{2,1,0:T(1,128)}), f32[32,1,128]{2,1,0:T(1,128)S(1)}, u32[]{:S(2)}, u32[]{:S(2)}) async-start(f32[32,1,128]{2,1,0:T(1,128)} %broadcast_in_dim.22), calls=%async_computation.2 | async-start | bytes 32768 | tf_op jit(solution)/shard_map/all_to_all | solution.py:145
  333.8 21.2 %all-to-all-done.2 = f32[32,1,128]{2,1,0:T(1,128)S(1)} async-done(((f32[32,1,128]{2,1,0:T(1,128)}), f32[32,1,128]{2,1,0:T(1,128)S(1)}, u32[]{:S(2)}, u32[]{:S(2)}) %all-to-all-start.2) | async-done | bytes 16416 | tf_op jit(solution)/shard_map/all_to_all | solution.py:145
  357.0 8.1 %all-to-all-start.3 = ((f32[32,2,128]{2,1,0:T(2,128)}), f32[32,2,128]{2,1,0:T(2,128)S(1)}, u32[]{:S(2)}, u32[]{:S(2)}) async-start(f32[32,2,128]{2,1,0:T(2,128)} %reshape.308), calls=%async_computation.3 | async-start | bytes 65536 | tf_op jit(solution)/shard_map/all_to_all | solution.py:151
  365.9 6.2 %all-to-all-done.3 = f32[32,2,128]{2,1,0:T(2,128)S(1)} async-done(((f32[32,2,128]{2,1,0:T(2,128)}), f32[32,2,128]{2,1,0:T(2,128)S(1)}, u32[]{:S(2)}, u32[]{:S(2)}) %all-to-all-start.3) | async-done | bytes 32800 | tf_op jit(solution)/shard_map/all_to_all | solution.py:151
  372.6 5.4 %fusion.20 = bf16[16,256,128]{2,1,0:T(8,128)(2,1)} fusion(s32[16,256]{1,0:T(8,128)S(1)} %iota_add_fusion, pred[16,256]{1,0:T(8,128)(4,1)S(1)} %copy-done.16, f32[16,256,128]{2,0,1:T(8,128)S(1)} %copy-done.8, bf16[16,256,128]{2,1,0:T(8,128)(2,1)} %copy-done.9, f32[16,256]{1,0:T(8,128)S(1)} %get-tuple-element.40, f32[16,256]{1,0:T(8,128)S(1)} %get-tuple-element.39), kind=kOutput, calls=%fused_computation.30 | convolution fusion | flops 273678336 | bytes 4247552 | tf_op jit(solution)/shard_map/krj,krd->kjd/dot_general | solution.py:181
  (156 shorter events, 53.4 us)
Async XLA Ops:
  7.2 21.1 %copy-start = (bf16[16,256,128]{2,1,0:T(8,128)(2,1)S(1)}, bf16[16,256,128]{2,1,0:T(8,128)(2,1)}, u32[]{:S(2)}) copy-start(bf16[16,256,128]{2,1,0:T(8,128)(2,1)} %param.8) | copy-start | bytes 3145732
  10.1 24.4 %all-to-all-start = ((s32[16,1,3]{2,1,0:T(1,128)}), s32[16,1,3]{2,1,0:T(1,128)S(1)}, u32[]{:S(2)}, u32[]{:S(2)}) async-start(s32[16,1,3]{2,1,0:T(1,128)} %copy.115), calls=%async_computation | async-start | bytes 16384 | tf_op jit(solution)/shard_map/all_to_all | solution.py:98
  28.3 3.9 %copy-start.15 = (pred[16,256]{1,0:T(8,128)(4,1)}, pred[16,256]{1,0:T(8,128)(4,1)S(1)}, u32[]{:S(2)}) copy-start(pred[16,256]{1,0:T(8,128)(4,1)S(1)} %iota_compare_fusion.1) | copy-start | bytes 12292
  32.6 8.7 %copy-start.14 = (f32[8192]{0:T(1024)S(1)}, f32[8192]{0:T(1024)}, u32[]{:S(2)}) copy-start(f32[8192]{0:T(1024)} %param.11) | copy-start | bytes 98308
  34.5 24.7 %all-to-all-start.1 = ((bf16[32,160,128]{2,1,0:T(8,128)(2,1)}), bf16[32,160,128]{2,1,0:T(8,128)(2,1)S(1)}, u32[]{:S(2)}, u32[]{:S(2)}) async-start(bf16[32,160,128]{2,1,0:T(8,128)(2,1)} %pad_maximum_fusion.2), calls=%async_computation.1 | async-start | bytes 2621440 | tf_op jit(solution)/shard_map/all_to_all | solution.py:109
  41.2 268.3 %reduce-scatter.4.cloned.1.call-start = ((), (), s32[]{:S(2)}) async-start(), calls=%async_computation.6 | async-start | bytes 5406720 | tf_op jit(solution)/shard_map/reduce_scatter | solution.py:138
  73.4 33.7 %collective-permute-start.1 = (bf16[72,512]{1,0:T(8,128)(2,1)S(1)}, bf16[72,512]{1,0:T(8,128)(2,1)S(1)}, u32[]{:S(2)}, u32[]{:S(2)}) collective-permute-start(bf16[72,512]{1,0:T(8,128)(2,1)S(1)} %get-tuple-element.38), channel_id=1, source_target_pairs={{0,48},{2,50},{4,52},{6,54},{8,56},{10,58},{12,60},{14,62},{16,0},... | collective-permute-start | bytes 221192 | tf_op jit(solution)/shard_map/ppermute | solution.py:33
  87.1 24.1 %collective-permute-start.2 = (bf16[72,512]{1,0:T(8,128)(2,1)S(1)}, bf16[72,512]{1,0:T(8,128)(2,1)S(1)}, u32[]{:S(2)}, u32[]{:S(2)}) collective-permute-start(bf16[72,512]{1,0:T(8,128)(2,1)S(1)} %get-tuple-element.38), channel_id=1, source_target_pairs={{0,32},{2,34},{4,36},{6,38},{8,40},{10,42},{12,44},{14,46},{16,48}... | collective-permute-start | bytes 221192 | tf_op jit(solution)/shard_map/ppermute | solution.py:33
  95.0 29.4 %collective-permute-start.3 = (bf16[72,512]{1,0:T(8,128)(2,1)S(1)}, bf16[72,512]{1,0:T(8,128)(2,1)S(1)}, u32[]{:S(2)}, u32[]{:S(2)}) collective-permute-start(bf16[72,512]{1,0:T(8,128)(2,1)S(1)} %get-tuple-element.38), channel_id=1, source_target_pairs={{0,16},{2,18},{4,20},{6,22},{8,24},{10,26},{12,28},{14,30},{16,32}... | collective-permute-start | bytes 221192 | tf_op jit(solution)/shard_map/ppermute | solution.py:33
  124.4 11.1 %collective-permute-start.7 = (bf16[4,72,512]{2,1,0:T(8,128)(2,1)S(1)}, bf16[4,72,512]{2,1,0:T(8,128)(2,1)S(1)}, u32[]{:S(2)}, u32[]{:S(2)}) collective-permute-start(bf16[4,72,512]{2,1,0:T(8,128)(2,1)S(1)} %get-tuple-element.30), channel_id=1, source_target_pairs={{0,4},{2,6},{4,8},{6,10},{8,12},{10,14},{12,16},{14,18},{16,20},{1... | collective-permute-start | bytes 884744 | tf_op jit(solution)/shard_map/ppermute | solution.py:33
  126.4 10.2 %collective-permute-start.4 = (bf16[4,72,512]{2,1,0:T(8,128)(2,1)S(1)}, bf16[4,72,512]{2,1,0:T(8,128)(2,1)S(1)}, u32[]{:S(2)}, u32[]{:S(2)}) collective-permute-start(bf16[4,72,512]{2,1,0:T(8,128)(2,1)S(1)} %get-tuple-element.30), channel_id=1, source_target_pairs={{0,60},{2,62},{4,0},{6,2},{8,4},{10,6},{12,8},{14,10},{16,12},{18,... | collective-permute-start | bytes 884744 | tf_op jit(solution)/shard_map/ppermute | solution.py:33
  136.7 37.7 %collective-permute-start.5 = (bf16[2,4,72,512]{3,2,1,0:T(8,128)(2,1)S(1)}, bf16[2,4,72,512]{3,2,1,0:T(8,128)(2,1)S(1)}, u32[]{:S(2)}, u32[]{:S(2)}) collective-permute-start(bf16[2,4,72,512]{3,2,1,0:T(8,128)(2,1)S(1)} %get-tuple-element.28), channel_id=1, source_target_pairs={{0,62},{2,0},{4,2},{6,4},{8,6},{10,8},{12,10},{14,12},{16,14},{18,... | collective-permute-start | bytes 1769480 | tf_op jit(solution)/shard_map/ppermute | solution.py:33
  152.5 41.1 %collective-permute-start.6 = (bf16[4,72,512]{2,1,0:T(8,128)(2,1)S(1)}, bf16[4,72,512]{2,1,0:T(8,128)(2,1)S(1)}, u32[]{:S(2)}, u32[]{:S(2)}) collective-permute-start(bf16[4,72,512]{2,1,0:T(8,128)(2,1)S(1)} %get-tuple-element.30), channel_id=1, source_target_pairs={{0,56},{2,58},{4,60},{6,62},{8,0},{10,2},{12,4},{14,6},{16,8},{18,... | collective-permute-start | bytes 884744 | tf_op jit(solution)/shard_map/ppermute | solution.py:33
  158.0 35.6 %collective-permute-start.8 = (bf16[2,4,72,512]{3,2,1,0:T(8,128)(2,1)S(1)}, bf16[2,4,72,512]{3,2,1,0:T(8,128)(2,1)S(1)}, u32[]{:S(2)}, u32[]{:S(2)}) collective-permute-start(bf16[2,4,72,512]{3,2,1,0:T(8,128)(2,1)S(1)} %get-tuple-element.27), channel_id=1, source_target_pairs={{0,2},{2,4},{4,6},{6,8},{8,10},{10,12},{12,14},{14,16},{16,18},{18... | collective-permute-start | bytes 1769480 | tf_op jit(solution)/shard_map/ppermute | solution.py:33
  195.0 27.2 %collective-permute-start.9 = (bf16[32,32,128]{2,0,1:T(8,128)(2,1)S(1)}, bf16[32,32,128]{2,0,1:T(8,128)(2,1)S(1)}, u32[]{:S(2)}, u32[]{:S(2)}) collective-permute-start(bf16[32,32,128]{2,0,1:T(8,128)(2,1)S(1)} %bitcast.182), channel_id=1, source_target_pairs={{0,512},{64,576},{128,640},{192,704},{256,768},{320,832},{384,896}... | collective-permute-start | bytes 786440 | tf_op jit(solution)/shard_map/ppermute | solution.py:12
  222.4 10.4 %collective-permute-start.10 = (bf16[2,32,32,128]{3,1,2,0:T(8,128)(2,1)S(1)}, bf16[2,32,32,128]{3,1,2,0:T(8,128)(2,1)}, u32[]{:S(2)}, u32[]{:S(2)}) collective-permute-start(bf16[2,32,32,128]{3,1,2,0:T(8,128)(2,1)S(1)} %pad_maximum_fusion.7), channel_id=1, source_target_pairs={{0,256},{64,320},{128,384},{192,448},{256,0},{320,64},{384,128},{4... | collective-permute-start | bytes 1572872 | tf_op jit(solution)/shard_map/ppermute | solution.py:12
  234.1 9.5 %copy-start.2 = (bf16[1,2,32,32,128]{4,2,3,1,0:T(8,128)(2,1)}, bf16[1,2,32,32,128]{4,2,3,1,0:T(8,128)(2,1)S(1)}, u32[]{:S(2)}) copy-start(bf16[1,2,32,32,128]{4,2,3,1,0:T(8,128)(2,1)S(1)} %get-tuple-element.23) | copy-start | bytes 1572868
  234.1 9.5 %copy-start.4 = (bf16[1,2,32,32,128]{4,2,3,1,0:T(8,128)(2,1)}, bf16[1,2,32,32,128]{4,2,3,1,0:T(8,128)(2,1)S(1)}, u32[]{:S(2)}) copy-start(bf16[1,2,32,32,128]{4,2,3,1,0:T(8,128)(2,1)S(1)} %get-tuple-element.24) | copy-start | bytes 1572868
  235.2 22.5 %collective-permute-start.11 = (bf16[2,2,32,32,128]{4,2,3,1,0:T(8,128)(2,1)}, bf16[2,2,32,32,128]{4,2,3,1,0:T(8,128)(2,1)}, u32[]{:S(2)}, u32[]{:S(2)}) collective-permute-start(bf16[2,2,32,32,128]{4,2,3,1,0:T(8,128)(2,1)} %pad_maximum_fusion.3), channel_id=1, source_target_pairs={{0,128},{64,192},{128,0},{192,64},{256,384},{320,448},{384,256},{4... | collective-permute-start | bytes 3145736 | tf_op jit(solution)/shard_map/ppermute | solution.py:12
  246.5 11.3 %copy-start.3 = (bf16[1,2,32,32,128]{4,2,3,1,0:T(8,128)(2,1)S(1)}, bf16[1,2,32,32,128]{4,2,3,1,0:T(8,128)(2,1)}, u32[]{:S(2)}) copy-start(bf16[1,2,32,32,128]{4,2,3,1,0:T(8,128)(2,1)} %copy-done.2) | copy-start | bytes 1572868
  246.5 11.3 %copy-start.5 = (bf16[1,2,32,32,128]{4,2,3,1,0:T(8,128)(2,1)S(1)}, bf16[1,2,32,32,128]{4,2,3,1,0:T(8,128)(2,1)}, u32[]{:S(2)}) copy-start(bf16[1,2,32,32,128]{4,2,3,1,0:T(8,128)(2,1)} %copy-done.4) | copy-start | bytes 1572868
  260.7 40.1 %collective-permute-start.12 = (bf16[2,2,2,32,32,128]{5,3,4,2,1,0:T(8,128)(2,1)}, bf16[2,2,2,32,32,128]{5,3,4,2,1,0:T(8,128)(2,1)}, u32[]{:S(2)}, u32[]{:S(2)}) collective-permute-start(bf16[2,2,2,32,32,128]{5,3,4,2,1,0:T(8,128)(2,1)} %pad_maximum_fusion.1), channel_id=1, source_target_pairs={{0,64},{64,0},{128,192},{192,128},{256,320},{320,256},{384,448},{4... | collective-permute-start | bytes 6291464 | tf_op jit(solution)/shard_map/ppermute | solution.py:12
  273.2 12.4 %copy-start.17 = (s32[16]{0:T(128)S(1)}, s32[16]{0:T(128)}, u32[]{:S(2)}) copy-start(s32[16]{0:T(128)} %get-tuple-element.41) | copy-start | bytes 196
  273.2 12.4 %copy-start.18 = (s32[16]{0:T(128)S(1)}, s32[16]{0:T(128)}, u32[]{:S(2)}) copy-start(s32[16]{0:T(128)} %get-tuple-element.42) | copy-start | bytes 196
  273.3 25.4 %all-to-all-start.4 = ((bf16[32,128,128]{2,1,0:T(8,128)(2,1)}), bf16[32,128,128]{2,1,0:T(8,128)(2,1)S(1)}, u32[]{:S(2)}, u32[]{:S(2)}) async-start(bf16[32,128,128]{2,1,0:T(8,128)(2,1)} %bitcast.173), calls=%async_computation.4 | async-start | bytes 2097152 | tf_op jit(solution)/shard_map/all_to_all | solution.py:169
  307.3 65.3 %copy-start.8 = (f32[16,256,128]{2,0,1:T(8,128)S(1)}, f32[16,256,128]{2,0,1:T(8,128)}, u32[]{:S(2)}) copy-start(f32[16,256,128]{2,0,1:T(8,128)} %fusion.28) | copy-start | bytes 6291460
  307.3 65.3 %copy-start.16 = (pred[16,256]{1,0:T(8,128)(4,1)S(1)}, pred[16,256]{1,0:T(8,128)(4,1)}, u32[]{:S(2)}) copy-start(pred[16,256]{1,0:T(8,128)(4,1)} %copy-done.15) | copy-start | bytes 12292
  307.4 57.8 %collective-permute-start.13 = (f32[128,256]{1,0:T(8,128)S(1)}, f32[128,256]{1,0:T(8,128)S(1)}, u32[]{:S(2)}, u32[]{:S(2)}) collective-permute-start(f32[128,256]{1,0:T(8,128)S(1)} %slice_select_fusion), channel_id=1, source_target_pairs={{0,1},{1,0},{2,3},{3,2},{4,5},{5,4},{6,7},{7,6},{8,9},{9,8},{10,11... | collective-permute-start | bytes 393224 | tf_op jit(solution)/shard_map/ppermute | solution.py:12
  311.4 22.4 %collective-permute-start = (bf16[64,256]{1,0:T(8,128)(2,1)S(1)}, bf16[64,256]{1,0:T(8,128)(2,1)S(1)}, u32[]{:S(2)}, u32[]{:S(2)}) collective-permute-start(bf16[64,256]{1,0:T(8,128)(2,1)S(1)} %broadcast_select_fusion.3), channel_id=1, source_target_pairs={{0,1},{1,0},{2,3},{3,2},{4,5},{5,4},{6,7},{7,6},{8,9},{9,8},{10,11... | collective-permute-start | bytes 98312 | tf_op jit(solution)/shard_map/ppermute | solution.py:12
  315.5 39.5 %all-to-all-start.2 = ((f32[32,1,128]{2,1,0:T(1,128)}), f32[32,1,128]{2,1,0:T(1,128)S(1)}, u32[]{:S(2)}, u32[]{:S(2)}) async-start(f32[32,1,128]{2,1,0:T(1,128)} %broadcast_in_dim.22), calls=%async_computation.2 | async-start | bytes 32768 | tf_op jit(solution)/shard_map/all_to_all | solution.py:145
  357.0 15.1 %all-to-all-start.3 = ((f32[32,2,128]{2,1,0:T(2,128)}), f32[32,2,128]{2,1,0:T(2,128)S(1)}, u32[]{:S(2)}, u32[]{:S(2)}) async-start(f32[32,2,128]{2,1,0:T(2,128)} %reshape.308), calls=%async_computation.3 | async-start | bytes 65536 | tf_op jit(solution)/shard_map/all_to_all | solution.py:151
  372.6 5.4 %copy-start.1 = (bf16[16,256,128]{2,1,0:T(8,128)(2,1)S(1)}, bf16[16,256,128]{2,1,0:T(8,128)(2,1)}, u32[]{:S(2)}) copy-start(bf16[16,256,128]{2,1,0:T(8,128)(2,1)} %param.8) | copy-start | bytes 3145732
  (7 other events, 10.1 us)
Sparse Core Ops, SparseCore 0:
  72.6 173.1 reduce-scatter.3
where the time goes:
time: 386 us; the launch traced here: 385 us
  starting transfers between devices  168 us (44%)
  waiting for transfers between devices  137 us (35%)
  other arithmetic  26 us (7%)
  local copies, waits for them, and re-layouts  20.9 us (5%)
  matrix products  18.3 us (5%)
  between operations  14.9 us (4%)
    ppermute x8, starting transfers between devices, fetched(): lax.ppermute(x, axis, [(i, (i - distance) % length) for i in range(length)])  64.3 us
    ppermute x8, waiting for transfers between devices, fetched(): lax.ppermute(x, axis, [(i, (i - distance) % length) for i in range(length)])  55.5 us
    ppermute x6, starting transfers between devices, swapped(): return lax.ppermute(x, axis, [(i, i ^ bit) for i in range(length)])  43.3 us
    ppermute x6, waiting for transfers between devices, swapped(): return lax.ppermute(x, axis, [(i, i ^ bit) for i in range(length)])  23.2 us
    all_to_all x1, waiting for transfers between devices, on_device(): lax.all_to_all(jnp.broadcast_to(scalars, (columns, 1, 2 * half_rows)), 'f...  21.2 us
    all_to_all x1, starting transfers between devices, on_device(): lax.all_to_all(jnp.broadcast_to(scalars, (columns, 1, 2 * half_rows)), 'f...  18.3 us
    all_to_all x1, starting transfers between devices, on_device(): lax.all_to_all(meta_out, 'section', split_axis=0, concat_axis=0, tiled=True)  17.4 us
    all_to_all x1, waiting for transfers between devices, on_device(): lax.all_to_all(jnp.concatenate([outgoing, w_copies], axis=1), plane, 0, 0...  17.2 us
  transfers between devices with their start and end apart: 20, of which 14 were waited for; matrix products, arithmetic and copies ran while one was open for 11% of the time, Pallas kernels for 0%

commit v1 on v0

--- a/solution.py
+++ b/solution.py
@@ -57,7 +57,7 @@
     columns = lax.axis_size("fsdp")
     pair_count = lax.axis_size("tp")
     tok_rows, feature_width = text_tokens.shape
-    img_count, most_slots, feature_slice = images.shape
+    _, most_slots, feature_slice = images.shape
     width = value_grad.shape[1]
     own_columns = value_weight.shape[1]
     half_width = width // pair_count
@@ -73,7 +73,6 @@
     own_half = lax.dynamic_index_in_dim(
         value_grad.reshape(pair_count, half_rows, width), pair_index, 0, keepdims=False
     )
-    own_half = lax.optimization_barrier(own_half)
     sent_rows = jnp.concatenate([own_half, w_rows_first.reshape(-1, width)])
     column_rows = gathered_by_windows(sent_rows, "fsdp")
     grads_in = column_rows[:, :half_rows]
@@ -132,38 +131,43 @@
         )
         for t in range(pair_count)
     )
+    image_raw = lax.psum_scatter(part, "fsdp", scatter_dimension=0, tiled=True)
+
+    grads_flat = grads_in.reshape(-1, width)
+    weighted = [
+        lax.dot_general(
+            grads_flat,
+            w_here[t],
+            (((1,), (0,)), ((), ())),
+            preferred_element_type=jnp.float32,
+        )
+        * gain_here[t]
+        for t in range(pair_count)
+    ]
     rows_f = [rows[t].astype(jnp.float32) for t in range(pair_count)]
-    squares = jnp.sum(sum(r * r for r in rows_f), axis=1, keepdims=True)
-    part = jnp.concatenate([part, jnp.broadcast_to(squares, (squares.shape[0], 128))], axis=1)
-    own_sums = lax.psum_scatter(part, "fsdp", scatter_dimension=0, tiled=True)
-    image_raw = own_sums[:, :width]
-    own_inv = lax.rsqrt(own_sums[:, width] / feature_width + epsilon)
-    own_inner = jnp.sum(image_raw * own_half.astype(jnp.float32), axis=1)
-    own_factor = own_inv * own_inv * own_inv * own_inner / feature_width
-
-    scalars = jnp.stack([own_inv, own_factor]).reshape(1, 1, -1)
-    scalars = lax.all_to_all(
-        jnp.broadcast_to(scalars, (columns, 1, 2 * half_rows)), "fsdp", 0, 0, tiled=True
-    )
-    scalars = scalars.reshape(sections, -1)
-    scalars = jnp.sum(order_int.astype(jnp.float32)[:, :, None] * scalars[None], axis=1)
-    scalars = jnp.broadcast_to(scalars[:, None], (sections, pair_count, scalars.shape[1]))
-    scalars = lax.all_to_all(scalars.reshape(sections * pair_count, 2, -1), plane, 0, 0, tiled=True)
-    scalars = scalars.reshape(1, sections, -1)
-    scalars = jnp.sum(routing.astype(jnp.float32)[:, :, None] * scalars, axis=1)
-    scalars = scalars.reshape(img_count, pair_count, halves, 2, half_rows).transpose(0, 3, 2, 1, 4)
-    scalars = scalars.reshape(img_count, 2, most_slots)
-
-    grads_flat = grads_in.reshape(-1, width)
+    sums = jnp.stack(
+        [
+            jnp.sum(sum(r * r for r in rows_f), axis=1),
+            jnp.sum(sum(w * r for w, r in zip(weighted, rows_f)), axis=1),
+        ]
+    )
+    sums = sums.reshape(2, columns, half_rows).transpose(1, 0, 2).reshape(columns, 1, -1)
+    sums_own = lax.all_to_all(sums, "fsdp", 0, 0, tiled=True)
+    sums_own = jnp.sum(sums_own, axis=0, keepdims=True)
+    sums_all = lax.all_to_all(
+        jnp.broadcast_to(sums_own, sums.shape), "fsdp", 0, 0, tiled=True
+    )
+    sums_all = sums_all.reshape(columns, 2, half_rows)
+    row_inv = lax.rsqrt(sums_all[:, 0].reshape(-1) / feature_width + epsilon)
+    row_factor = row_inv * row_inv * row_inv * sums_all[:, 1].reshape(-1) / feature_width
     by_source = []
     for t in range(pair_count):
-        weighted = lax.dot_general(
-            grads_flat, w_here[t], (((1,), (0,)), ((), ())), preferred_element_type=jnp.float32
-        )
-        weighted = (weighted * gain_here[t]).astype(jnp.bfloat16)
-        weighted = weighted.reshape(sections, halves * half_rows, feature_slice)
+        grad_rows = (
+            row_inv[:, None] * weighted[t] - rows_f[t] * row_factor[:, None]
+        ).astype(jnp.bfloat16)
+        grad_rows = grad_rows.reshape(sections, halves * half_rows, feature_slice)
         by_source.append(
-            jnp.einsum("sr,rpd->spd", order_float, weighted, preferred_element_type=jnp.float32)
+            jnp.einsum("sr,rpd->spd", order_float, grad_rows, preferred_element_type=jnp.float32)
         )
     by_source = jnp.stack(by_source, axis=1).astype(jnp.bfloat16)
     returned = lax.all_to_all(
@@ -171,15 +175,11 @@
     )
     returned = returned.reshape(sections, pair_count, halves, half_rows, feature_slice)
     returned = returned.transpose(0, 2, 1, 3, 4).reshape(sections, most_slots, feature_slice)
-    own_weighted = jnp.einsum(
+    own_rows = jnp.einsum(
         "kt,trd->krd", route_float, returned, preferred_element_type=jnp.float32
-    )
-    grad_rows = (
-        scalars[:, 0, :, None] * own_weighted
-        - placed.astype(jnp.float32) * scalars[:, 1, :, None]
     ).astype(jnp.bfloat16)
     visual_grads = jnp.einsum(
-        "krj,krd->kjd", placing, grad_rows, preferred_element_type=jnp.float32
+        "krj,krd->kjd", placing, own_rows, preferred_element_type=jnp.float32
     ).astype(jnp.bfloat16)
 
     w_all = gathered_by_bits(w_column.transpose(1, 0, 2), "section").reshape(width, -1)
@@ -200,6 +200,7 @@
     text_got = swapped(text_sent, "tp", 1)
     text_values = ((text_kept + text_got) * text_inv).astype(jnp.bfloat16)
 
+    own_inv = lax.rsqrt(sums_own.reshape(2, half_rows)[0] / feature_width + epsilon)
     image_values = (image_raw * own_inv[:, None]).astype(jnp.bfloat16)
     image_kept = jnp.where(is_second, image_values[:, half_width:], image_values[:, :half_width])
     image_sent = jnp.where(is_second, image_values[:, :half_width], image_values[:, half_width:])

time: 386 us -> 326 us (0.84)
  waiting for transfers between devices: 137 us -> 88.8 us
  starting transfers between devices: 168 us -> 147 us
  local copies, waits for them, and re-layouts: 20.9 us -> 27.3 us
    ppermute x8, waiting for transfers between devices: 55.5 us -> 22.6 us  [fetched(): lax.ppermute(x, axis, [(i, (i - distance) % length) for i in range(length)])]
    ppermute x6, starting transfers between devices: 43.3 us -> 24.7 us  [swapped(): return lax.ppermute(x, axis, [(i, i ^ bit) for i in range(length)])]
    all_to_all x1, waiting for transfers between devices: 17.2 us -> 0.01 us  [on_device(): lax.all_to_all(jnp.concatenate([outgoing, w_copies], axis=1), plane, 0, 0...]
    all_to_all x1, starting transfers between devices: 17.4 us -> 8.46 us  [on_device(): lax.all_to_all(meta_out, 'section', split_axis=0, concat_axis=0, tiled=True)]
    ppermute x8, starting transfers between devices: 64.3 us -> 72.9 us  [fetched(): lax.ppermute(x, axis, [(i, (i - distance) % length) for i in range(length)])]
    all_to_all x2, waiting for transfers between devices: 27.4 us -> 35.8 us  [the longest x1 19 us: on_device(): sums_own = lax.all_to_all(sums, 'fsdp', 0, 0, tiled=True)]
    ppermute x6, waiting for transfers between devices: 23.2 us -> 17.4 us  [swapped(): return lax.ppermute(x, axis, [(i, i ^ bit) for i in range(length)])]
    all_to_all x1, starting transfers between devices: 9.79 us -> 5.55 us  [on_device(): lax.all_to_all(by_source.reshape(-1, halves * half_rows, feature_slice),...]
  transfers between devices with their start and end apart: 20 -> 20, of which waited for: 14 -> 9; matrix products, arithmetic and copies ran while one was open for 11% -> 21% of each run, Pallas kernels for 0% -> 0%
where the time goes in v1:
time: 326 us; the launch traced here: 322 us
  starting transfers between devices  147 us (45%)
  waiting for transfers between devices  88.8 us (27%)
  local copies, waits for them, and re-layouts  27.3 us (8%)
  other arithmetic  27.2 us (8%)
  matrix products  17.4 us (5%)
  between operations  14.8 us (5%)
    ppermute x8, starting transfers between devices, fetched(): lax.ppermute(x, axis, [(i, (i - distance) % length) for i in range(length)])  72.9 us
    ppermute x6, starting transfers between devices, swapped(): return lax.ppermute(x, axis, [(i, i ^ bit) for i in range(length)])  24.7 us
    ppermute x8, waiting for transfers between devices, fetched(): lax.ppermute(x, axis, [(i, (i - distance) % length) for i in range(length)])  22.6 us
    all_to_all x1, starting transfers between devices, on_device(): sums_own = lax.all_to_all(sums, 'fsdp', 0, 0, tiled=True)  22.4 us
    all_to_all x1, waiting for transfers between devices, on_device(): sums_own = lax.all_to_all(sums, 'fsdp', 0, 0, tiled=True)  19 us
    ppermute x6, waiting for transfers between devices, swapped(): return lax.ppermute(x, axis, [(i, i ^ bit) for i in range(length)])  17.4 us
    all_to_all x1, waiting for transfers between devices, on_device(): lax.all_to_all(jnp.broadcast_to(sums_own, sums.shape), 'fsdp', 0, 0, tile...  16.9 us
    all_to_all x1, waiting for transfers between devices, on_device(): lax.all_to_all(by_source.reshape(-1, halves * half_rows, feature_slice),...  12.8 us
  transfers between devices with their start and end apart: 20, of which 9 were waited for; matrix products, arithmetic and copies ran while one was open for 21% of the time, Pallas kernels for 0%

profile of v1, /device:TPU:1, one launch (start us, length us, event | category | flops | bytes accessed | tf_op | source)
XLA Modules:
  0.0 322.3 jit_solution(16056861067710978572)
XLA Ops:
  8.9 23.5 %collective-permute-start = (bf16[72,512]{1,0:T(8,128)(2,1)S(1)}, bf16[72,512]{1,0:T(8,128)(2,1)S(1)}, u32[]{:S(2)}, u32[]{:S(2)}) collective-permute-start(bf16[72,512]{1,0:T(8,128)(2,1)S(1)} %get-tuple-element.32), channel_id=1, source_target_pairs={{0,48},{2,50},{4,52},{6,54},{8,56},{10,58},{12,60},{14,62},{16,0},... | collective-permute-start | bytes 221192 | tf_op jit(solution)/shard_map/ppermute | solution.py:33
  32.4 7.9 %collective-permute-start.1 = (bf16[72,512]{1,0:T(8,128)(2,1)S(1)}, bf16[72,512]{1,0:T(8,128)(2,1)S(1)}, u32[]{:S(2)}, u32[]{:S(2)}) collective-permute-start(bf16[72,512]{1,0:T(8,128)(2,1)S(1)} %get-tuple-element.32), channel_id=1, source_target_pairs={{0,32},{2,34},{4,36},{6,38},{8,40},{10,42},{12,44},{14,46},{16,48}... | collective-permute-start | bytes 221192 | tf_op jit(solution)/shard_map/ppermute | solution.py:33
  40.3 12.1 %collective-permute-start.2 = (bf16[72,512]{1,0:T(8,128)(2,1)S(1)}, bf16[72,512]{1,0:T(8,128)(2,1)S(1)}, u32[]{:S(2)}, u32[]{:S(2)}) collective-permute-start(bf16[72,512]{1,0:T(8,128)(2,1)S(1)} %get-tuple-element.32), channel_id=1, source_target_pairs={{0,16},{2,18},{4,20},{6,22},{8,24},{10,26},{12,28},{14,30},{16,32}... | collective-permute-start | bytes 221192 | tf_op jit(solution)/shard_map/ppermute | solution.py:33
  55.2 8.5 %all-to-all-start = ((s32[16,1,3]{2,1,0:T(1,128)}), s32[16,1,3]{2,1,0:T(1,128)S(1)}, u32[]{:S(2)}, u32[]{:S(2)}) async-start(s32[16,1,3]{2,1,0:T(1,128)} %copy.129), calls=%async_computation | async-start | bytes 16384 | tf_op jit(solution)/shard_map/all_to_all | solution.py:97
  68.9 3.0 fusion.13
  72.0 5.5 %collective-permute-start.3 = (bf16[4,72,512]{2,1,0:T(8,128)(2,1)}, bf16[4,72,512]{2,1,0:T(8,128)(2,1)S(1)}, u32[]{:S(2)}, u32[]{:S(2)}) collective-permute-start(bf16[4,72,512]{2,1,0:T(8,128)(2,1)} %get-tuple-element.26), channel_id=1, source_target_pairs={{0,60},{2,62},{4,0},{6,2},{8,4},{10,6},{12,8},{14,10},{16,12},{18,... | collective-permute-start | bytes 884744 | tf_op jit(solution)/shard_map/ppermute | solution.py:33
  82.6 14.6 %collective-permute-start.4 = (bf16[2,4,72,512]{3,2,1,0:T(8,128)(2,1)}, bf16[2,4,72,512]{3,2,1,0:T(8,128)(2,1)S(1)}, u32[]{:S(2)}, u32[]{:S(2)}) collective-permute-start(bf16[2,4,72,512]{3,2,1,0:T(8,128)(2,1)} %get-tuple-element.24), channel_id=1, source_target_pairs={{0,62},{2,0},{4,2},{6,4},{8,6},{10,8},{12,10},{14,12},{16,14},{18,... | collective-permute-start | bytes 1769480 | tf_op jit(solution)/shard_map/ppermute | solution.py:33
  99.6 9.0 %all-to-all-start.1 = ((bf16[32,160,128]{2,1,0:T(8,128)(2,1)}), bf16[32,160,128]{2,1,0:T(8,128)(2,1)S(1)}, u32[]{:S(2)}, u32[]{:S(2)}) async-start(bf16[32,160,128]{2,1,0:T(8,128)(2,1)} %pad_maximum_fusion.2), calls=%async_computation.1 | async-start | bytes 2621440 | tf_op jit(solution)/shard_map/all_to_all | solution.py:108
  108.7 5.6 %collective-permute-start.5 = (bf16[4,72,512]{2,1,0:T(8,128)(2,1)}, bf16[4,72,512]{2,1,0:T(8,128)(2,1)S(1)}, u32[]{:S(2)}, u32[]{:S(2)}) collective-permute-start(bf16[4,72,512]{2,1,0:T(8,128)(2,1)} %get-tuple-element.26), channel_id=1, source_target_pairs={{0,56},{2,58},{4,60},{6,62},{8,0},{10,2},{12,4},{14,6},{16,8},{18,... | collective-permute-start | bytes 884744 | tf_op jit(solution)/shard_map/ppermute | solution.py:33
  119.3 20.0 %collective-permute-done.5 = bf16[4,72,512]{2,1,0:T(8,128)(2,1)S(1)} collective-permute-done((bf16[4,72,512]{2,1,0:T(8,128)(2,1)}, bf16[4,72,512]{2,1,0:T(8,128)(2,1)S(1)}, u32[]{:S(2)}, u32[]{:S(2)}) %collective-permute-start.5) | collective-permute-done | bytes 294944 | tf_op jit(solution)/shard_map/ppermute | solution.py:33
  144.1 2.7 convolution_add_fusion
  151.9 2.5 fusion.8
  158.7 4.6 %collective-permute-start.9 = (bf16[32,32,128]{2,1,0:T(8,128)(2,1)}, bf16[32,32,128]{2,1,0:T(8,128)(2,1)}, u32[]{:S(2)}, u32[]{:S(2)}) collective-permute-start(bf16[32,32,128]{2,1,0:T(8,128)(2,1)} %bitcast.180), channel_id=1, source_target_pairs={{0,512},{64,576},{128,640},{192,704},{256,768},{320,832},{384,896}... | collective-permute-start | bytes 786440 | tf_op jit(solution)/shard_map/ppermute | solution.py:12
  163.7 6.1 %collective-permute-done.9 = bf16[32,32,128]{2,1,0:T(8,128)(2,1)} collective-permute-done((bf16[32,32,128]{2,1,0:T(8,128)(2,1)}, bf16[32,32,128]{2,1,0:T(8,128)(2,1)}, u32[]{:S(2)}, u32[]{:S(2)}) %collective-permute-start.9) | collective-permute-done | bytes 262176 | tf_op jit(solution)/shard_map/ppermute | solution.py:12
  171.0 3.2 collective-permute-start.10
  176.7 8.6 %collective-permute-done.10 = bf16[2,32,32,128]{3,2,1,0:T(8,128)(2,1)S(1)} collective-permute-done((bf16[2,32,32,128]{3,2,1,0:T(8,128)(2,1)S(1)}, bf16[2,32,32,128]{3,2,1,0:T(8,128)(2,1)S(1)}, u32[]{:S(2)}, u32[]{:S(2)}) %collective-permute-start.10) | collective-permute-done | bytes 524320 | tf_op jit(solution)/shard_map/ppermute | solution.py:12
  185.5 4.6 %collective-permute-start.11 = (bf16[2,2,32,32,128]{4,3,2,0,1:T(8,128)(2,1)S(1)}, bf16[2,2,32,32,128]{4,3,2,0,1:T(8,128)(2,1)}, u32[]{:S(2)}, u32[]{:S(2)}) collective-permute-start(bf16[2,2,32,32,128]{4,3,2,0,1:T(8,128)(2,1)S(1)} %pad_maximum_fusion.3), channel_id=1, source_target_pairs={{0,128},{64,192},{128,0},{192,64},{256,384},{320,448},{384,256},{4... | collective-permute-start | bytes 3145736 | tf_op jit(solution)/shard_map/ppermute | solution.py:12
  191.4 22.4 %all-to-all-start.2 = ((f32[32,1,128]{2,1,0:T(1,128)}), f32[32,1,128]{2,1,0:T(1,128)S(1)}, u32[]{:S(2)}, u32[]{:S(2)}) async-start(f32[32,1,128]{2,1,0:T(1,128)} %bitcast.57), calls=%async_computation.3 | async-start | bytes 32768 | tf_op jit(solution)/shard_map/all_to_all | solution.py:155
  213.8 2.1 multiply_reduce_fusion
  215.9 19.0 %all-to-all-done.2 = f32[32,1,128]{2,1,0:T(1,128)S(1)} async-done(((f32[32,1,128]{2,1,0:T(1,128)}), f32[32,1,128]{2,1,0:T(1,128)S(1)}, u32[]{:S(2)}, u32[]{:S(2)}) %all-to-all-start.2) | async-done | bytes 16416 | tf_op jit(solution)/shard_map/all_to_all | solution.py:155
  235.5 3.8 %all-to-all-start.3 = ((f32[32,1,128]{2,1,0:T(1,128)}), f32[32,1,128]{2,1,0:T(1,128)S(1)}, u32[]{:S(2)}, u32[]{:S(2)}) async-start(f32[32,1,128]{2,1,0:T(1,128)} %broadcast_in_dim.11), calls=%async_computation.4 | async-start | bytes 32768 | tf_op jit(solution)/shard_map/all_to_all | solution.py:157
  239.3 4.1 %copy.150 = bf16[128,8192]{0,1:T(8,128)(2,1)} copy(bf16[128,8192]{1,0:T(8,128)(2,1)} %param.7) | data formatting | bytes 4194304 | tf_op args[0]
  243.5 16.9 %all-to-all-done.3 = f32[32,1,128]{2,1,0:T(1,128)S(1)} async-done(((f32[32,1,128]{2,1,0:T(1,128)}), f32[32,1,128]{2,1,0:T(1,128)S(1)}, u32[]{:S(2)}, u32[]{:S(2)}) %all-to-all-start.3) | async-done | bytes 16416 | tf_op jit(solution)/shard_map/all_to_all | solution.py:157
  265.2 7.0 %collective-permute-start.12 = (bf16[2,2,2,32,32,128]{5,4,3,0,1,2:T(8,128)(2,1)}, bf16[2,2,2,32,32,128]{5,4,3,0,1,2:T(8,128)(2,1)}, u32[]{:S(2)}, u32[]{:S(2)}) collective-permute-start(bf16[2,2,2,32,32,128]{5,4,3,0,1,2:T(8,128)(2,1)} %pad_maximum_fusion.1), channel_id=1, source_target_pairs={{0,64},{64,0},{128,192},{192,128},{256,320},{320,256},{384,448},{4... | collective-permute-start | bytes 6291464 | tf_op jit(solution)/shard_map/ppermute | solution.py:12
  275.2 5.5 %all-to-all-start.4 = ((bf16[32,128,128]{2,1,0:T(8,128)(2,1)}), bf16[32,128,128]{2,1,0:T(8,128)(2,1)S(1)}, u32[]{:S(2)}, u32[]{:S(2)}) async-start(bf16[32,128,128]{2,1,0:T(8,128)(2,1)} %bitcast.192), calls=%async_computation.5 | async-start | bytes 2097152 | tf_op jit(solution)/shard_map/all_to_all | solution.py:173
  280.8 2.5 multiply_convert_fusion
  283.6 12.8 %all-to-all-done.4 = bf16[32,128,128]{2,1,0:T(8,128)(2,1)S(1)} async-done(((bf16[32,128,128]{2,1,0:T(8,128)(2,1)}), bf16[32,128,128]{2,1,0:T(8,128)(2,1)S(1)}, u32[]{:S(2)}, u32[]{:S(2)}) %all-to-all-start.4) | async-done | bytes 1048608 | tf_op jit(solution)/shard_map/all_to_all | solution.py:173
  297.3 2.9 fusion.16
  303.2 2.4 fusion
  306.7 1.9 collective-permute-start.8
  308.7 3.4 %collective-permute-start.13 = (f32[128,256]{1,0:T(8,128)S(1)}, f32[128,256]{1,0:T(8,128)S(1)}, u32[]{:S(2)}, u32[]{:S(2)}) collective-permute-start(f32[128,256]{1,0:T(8,128)S(1)} %slice_select_fusion), channel_id=1, source_target_pairs={{0,1},{1,0},{2,3},{3,2},{4,5},{5,4},{6,7},{7,6},{8,9},{9,8},{10,11... | collective-permute-start | bytes 393224 | tf_op jit(solution)/shard_map/ppermute | solution.py:12
  312.1 2.7 collective-permute-done.13
  (157 shorter events, 56.2 us)
Async XLA Ops:
  7.2 61.8 %copy-start = (bf16[16,256,128]{2,1,0:T(8,128)(2,1)S(1)}, bf16[16,256,128]{2,1,0:T(8,128)(2,1)}, u32[]{:S(2)}) copy-start(bf16[16,256,128]{2,1,0:T(8,128)(2,1)} %param.8) | copy-start | bytes 3145732
  8.9 55.7 %collective-permute-start = (bf16[72,512]{1,0:T(8,128)(2,1)S(1)}, bf16[72,512]{1,0:T(8,128)(2,1)S(1)}, u32[]{:S(2)}, u32[]{:S(2)}) collective-permute-start(bf16[72,512]{1,0:T(8,128)(2,1)S(1)} %get-tuple-element.32), channel_id=1, source_target_pairs={{0,48},{2,50},{4,52},{6,54},{8,56},{10,58},{12,60},{14,62},{16,0},... | collective-permute-start | bytes 221192 | tf_op jit(solution)/shard_map/ppermute | solution.py:33
  32.4 32.1 %collective-permute-start.1 = (bf16[72,512]{1,0:T(8,128)(2,1)S(1)}, bf16[72,512]{1,0:T(8,128)(2,1)S(1)}, u32[]{:S(2)}, u32[]{:S(2)}) collective-permute-start(bf16[72,512]{1,0:T(8,128)(2,1)S(1)} %get-tuple-element.32), channel_id=1, source_target_pairs={{0,32},{2,34},{4,36},{6,38},{8,40},{10,42},{12,44},{14,46},{16,48}... | collective-permute-start | bytes 221192 | tf_op jit(solution)/shard_map/ppermute | solution.py:33
  40.3 25.9 %collective-permute-start.2 = (bf16[72,512]{1,0:T(8,128)(2,1)S(1)}, bf16[72,512]{1,0:T(8,128)(2,1)S(1)}, u32[]{:S(2)}, u32[]{:S(2)}) collective-permute-start(bf16[72,512]{1,0:T(8,128)(2,1)S(1)} %get-tuple-element.32), channel_id=1, source_target_pairs={{0,16},{2,18},{4,20},{6,22},{8,24},{10,26},{12,28},{14,30},{16,32}... | collective-permute-start | bytes 221192 | tf_op jit(solution)/shard_map/ppermute | solution.py:33
  53.7 23.8 %copy-start.18 = (s32[16]{0:T(128)}, s32[16]{0:T(128)S(1)}, u32[]{:S(2)}) copy-start(s32[16]{0:T(128)S(1)} %get-tuple-element.43) | copy-start | bytes 196
  55.2 44.4 %all-to-all-start = ((s32[16,1,3]{2,1,0:T(1,128)}), s32[16,1,3]{2,1,0:T(1,128)S(1)}, u32[]{:S(2)}, u32[]{:S(2)}) async-start(s32[16,1,3]{2,1,0:T(1,128)} %copy.129), calls=%async_computation | async-start | bytes 16384 | tf_op jit(solution)/shard_map/all_to_all | solution.py:97
  67.0 11.6 %collective-permute-start.6 = (bf16[4,72,512]{2,1,0:T(8,128)(2,1)}, bf16[4,72,512]{2,1,0:T(8,128)(2,1)}, u32[]{:S(2)}, u32[]{:S(2)}) collective-permute-start(bf16[4,72,512]{2,1,0:T(8,128)(2,1)} %get-tuple-element.26), channel_id=1, source_target_pairs={{0,4},{2,6},{4,8},{6,10},{8,12},{10,14},{12,16},{14,18},{16,20},{1... | collective-permute-start | bytes 884744 | tf_op jit(solution)/shard_map/ppermute | solution.py:33
  72.0 9.4 %collective-permute-start.3 = (bf16[4,72,512]{2,1,0:T(8,128)(2,1)}, bf16[4,72,512]{2,1,0:T(8,128)(2,1)S(1)}, u32[]{:S(2)}, u32[]{:S(2)}) collective-permute-start(bf16[4,72,512]{2,1,0:T(8,128)(2,1)} %get-tuple-element.26), channel_id=1, source_target_pairs={{0,60},{2,62},{4,0},{6,2},{8,4},{10,6},{12,8},{14,10},{16,12},{18,... | collective-permute-start | bytes 884744 | tf_op jit(solution)/shard_map/ppermute | solution.py:33
  78.3 20.1 %copy-start.14 = (bf16[128,32]{0,1:T(8,128)(2,1)S(1)}, bf16[128,32]{0,1:T(8,128)(2,1)}, u32[]{:S(2)}) copy-start(bf16[128,32]{0,1:T(8,128)(2,1)} %param.12) | copy-start | bytes 24580
  82.6 34.4 %collective-permute-start.4 = (bf16[2,4,72,512]{3,2,1,0:T(8,128)(2,1)}, bf16[2,4,72,512]{3,2,1,0:T(8,128)(2,1)S(1)}, u32[]{:S(2)}, u32[]{:S(2)}) collective-permute-start(bf16[2,4,72,512]{3,2,1,0:T(8,128)(2,1)} %get-tuple-element.24), channel_id=1, source_target_pairs={{0,62},{2,0},{4,2},{6,4},{8,6},{10,8},{12,10},{14,12},{16,14},{18,... | collective-permute-start | bytes 1769480 | tf_op jit(solution)/shard_map/ppermute | solution.py:33
  99.6 40.4 %all-to-all-start.1 = ((bf16[32,160,128]{2,1,0:T(8,128)(2,1)}), bf16[32,160,128]{2,1,0:T(8,128)(2,1)S(1)}, u32[]{:S(2)}, u32[]{:S(2)}) async-start(bf16[32,160,128]{2,1,0:T(8,128)(2,1)} %pad_maximum_fusion.2), calls=%async_computation.1 | async-start | bytes 2621440 | tf_op jit(solution)/shard_map/all_to_all | solution.py:108
  108.6 197.1 %reduce-scatter.2.cloned.1.call-start = ((), (), s32[]{:S(2)}) async-start(), calls=%async_computation.6 | async-start | bytes 4325376 | tf_op jit(solution)/shard_map/reduce_scatter | solution.py:134
  108.7 30.5 %collective-permute-start.5 = (bf16[4,72,512]{2,1,0:T(8,128)(2,1)}, bf16[4,72,512]{2,1,0:T(8,128)(2,1)S(1)}, u32[]{:S(2)}, u32[]{:S(2)}) collective-permute-start(bf16[4,72,512]{2,1,0:T(8,128)(2,1)} %get-tuple-element.26), channel_id=1, source_target_pairs={{0,56},{2,58},{4,60},{6,62},{8,0},{10,2},{12,4},{14,6},{16,8},{18,... | collective-permute-start | bytes 884744 | tf_op jit(solution)/shard_map/ppermute | solution.py:33
  115.1 31.8 %collective-permute-start.7 = (bf16[2,4,72,512]{3,2,1,0:T(8,128)(2,1)}, bf16[2,4,72,512]{3,2,1,0:T(8,128)(2,1)}, u32[]{:S(2)}, u32[]{:S(2)}) collective-permute-start(bf16[2,4,72,512]{3,2,1,0:T(8,128)(2,1)} %get-tuple-element.23), channel_id=1, source_target_pairs={{0,2},{2,4},{4,6},{6,8},{8,10},{10,12},{12,14},{14,16},{16,18},{18... | collective-permute-start | bytes 1769480 | tf_op jit(solution)/shard_map/ppermute | solution.py:33
  151.9 11.5 %copy-start.17 = (f32[8192]{0:T(1024)S(1)}, f32[8192]{0:T(1024)}, u32[]{:S(2)}) copy-start(f32[8192]{0:T(1024)} %param.11) | copy-start | bytes 98308
  158.7 11.1 %collective-permute-start.9 = (bf16[32,32,128]{2,1,0:T(8,128)(2,1)}, bf16[32,32,128]{2,1,0:T(8,128)(2,1)}, u32[]{:S(2)}, u32[]{:S(2)}) collective-permute-start(bf16[32,32,128]{2,1,0:T(8,128)(2,1)} %bitcast.180), channel_id=1, source_target_pairs={{0,512},{64,576},{128,640},{192,704},{256,768},{320,832},{384,896}... | collective-permute-start | bytes 786440 | tf_op jit(solution)/shard_map/ppermute | solution.py:12
  163.4 10.8 %copy-start.13 = (bf16[2,16,32,128]{3,2,0,1:T(8,128)(2,1)S(1)}, bf16[2,16,32,128]{3,2,0,1:T(8,128)(2,1)}, u32[]{:S(2)}) copy-start(bf16[2,16,32,128]{3,2,0,1:T(8,128)(2,1)} %get-tuple-element.15) | copy-start | bytes 786436
  171.0 14.3 %collective-permute-start.10 = (bf16[2,32,32,128]{3,2,1,0:T(8,128)(2,1)S(1)}, bf16[2,32,32,128]{3,2,1,0:T(8,128)(2,1)S(1)}, u32[]{:S(2)}, u32[]{:S(2)}) collective-permute-start(bf16[2,32,32,128]{3,2,1,0:T(8,128)(2,1)S(1)} %pad_maximum_fusion.7), channel_id=1, source_target_pairs={{0,256},{64,320},{128,384},{192,448},{256,0},{320,64},{384,128},{4... | collective-permute-start | bytes 1572872 | tf_op jit(solution)/shard_map/ppermute | solution.py:12
  185.5 76.4 %collective-permute-start.11 = (bf16[2,2,32,32,128]{4,3,2,0,1:T(8,128)(2,1)S(1)}, bf16[2,2,32,32,128]{4,3,2,0,1:T(8,128)(2,1)}, u32[]{:S(2)}, u32[]{:S(2)}) collective-permute-start(bf16[2,2,32,32,128]{4,3,2,0,1:T(8,128)(2,1)S(1)} %pad_maximum_fusion.3), channel_id=1, source_target_pairs={{0,128},{64,192},{128,0},{192,64},{256,384},{320,448},{384,256},{4... | collective-permute-start | bytes 3145736 | tf_op jit(solution)/shard_map/ppermute | solution.py:12
  191.4 43.4 %all-to-all-start.2 = ((f32[32,1,128]{2,1,0:T(1,128)}), f32[32,1,128]{2,1,0:T(1,128)S(1)}, u32[]{:S(2)}, u32[]{:S(2)}) async-start(f32[32,1,128]{2,1,0:T(1,128)} %bitcast.57), calls=%async_computation.3 | async-start | bytes 32768 | tf_op jit(solution)/shard_map/all_to_all | solution.py:155
  235.5 24.8 %all-to-all-start.3 = ((f32[32,1,128]{2,1,0:T(1,128)}), f32[32,1,128]{2,1,0:T(1,128)S(1)}, u32[]{:S(2)}, u32[]{:S(2)}) async-start(f32[32,1,128]{2,1,0:T(1,128)} %broadcast_in_dim.11), calls=%async_computation.4 | async-start | bytes 32768 | tf_op jit(solution)/shard_map/all_to_all | solution.py:157
  263.6 8.6 %copy-start.4 = (bf16[1,16,128,128]{3,2,1,0:T(8,128)(2,1)S(1)}, bf16[1,16,128,128]{3,2,1,0:T(8,128)(2,1)}, u32[]{:S(2)}) copy-start(bf16[1,16,128,128]{3,2,1,0:T(8,128)(2,1)} %copy-done.2) | copy-start | bytes 1572868
  263.6 8.6 %copy-start.7 = (bf16[1,16,128,128]{3,2,1,0:T(8,128)(2,1)S(1)}, bf16[1,16,128,128]{3,2,1,0:T(8,128)(2,1)}, u32[]{:S(2)}) copy-start(bf16[1,16,128,128]{3,2,1,0:T(8,128)(2,1)} %copy-done.5) | copy-start | bytes 1572868
  263.6 8.6 %copy-start.10 = (f32[2048,128]{1,0:T(8,128)S(1)}, f32[2048,128]{1,0:T(8,128)}, u32[]{:S(2)}) copy-start(f32[2048,128]{1,0:T(8,128)} %get-tuple-element.41) | copy-start | bytes 3145732
  265.2 35.0 %collective-permute-start.12 = (bf16[2,2,2,32,32,128]{5,4,3,0,1,2:T(8,128)(2,1)}, bf16[2,2,2,32,32,128]{5,4,3,0,1,2:T(8,128)(2,1)}, u32[]{:S(2)}, u32[]{:S(2)}) collective-permute-start(bf16[2,2,2,32,32,128]{5,4,3,0,1,2:T(8,128)(2,1)} %pad_maximum_fusion.1), channel_id=1, source_target_pairs={{0,64},{64,0},{128,192},{192,128},{256,320},{320,256},{384,448},{4... | collective-permute-start | bytes 6291464 | tf_op jit(solution)/shard_map/ppermute | solution.py:12
  275.2 21.2 %all-to-all-start.4 = ((bf16[32,128,128]{2,1,0:T(8,128)(2,1)}), bf16[32,128,128]{2,1,0:T(8,128)(2,1)S(1)}, u32[]{:S(2)}, u32[]{:S(2)}) async-start(bf16[32,128,128]{2,1,0:T(8,128)(2,1)} %bitcast.192), calls=%async_computation.5 | async-start | bytes 2097152 | tf_op jit(solution)/shard_map/all_to_all | solution.py:173
  280.8 15.7 %copy-start.19 = (s32[16]{0:T(128)S(1)}, s32[16]{0:T(128)}, u32[]{:S(2)}) copy-start(s32[16]{0:T(128)} %copy-done.18) | copy-start | bytes 196
  283.3 13.9 %copy-start.16 = (s32[16,256]{1,0:T(8,128)S(1)}, s32[16,256]{1,0:T(8,128)}, u32[]{:S(2)}) copy-start(s32[16,256]{1,0:T(8,128)} %copy-done.15) | copy-start | bytes 49156
  283.3 13.9 %copy-start.22 = (pred[16,256]{1,0:T(8,128)(4,1)S(1)}, pred[16,256]{1,0:T(8,128)(4,1)}, u32[]{:S(2)}) copy-start(pred[16,256]{1,0:T(8,128)(4,1)} %copy-done.21) | copy-start | bytes 12292
  302.4 13.1 %copy-start.1 = (bf16[16,256,128]{2,1,0:T(8,128)(2,1)S(1)}, bf16[16,256,128]{2,1,0:T(8,128)(2,1)}, u32[]{:S(2)}) copy-start(bf16[16,256,128]{2,1,0:T(8,128)(2,1)} %param.8) | copy-start | bytes 3145732
  306.7 5.3 %collective-permute-start.8 = (bf16[64,256]{1,0:T(8,128)(2,1)S(1)}, bf16[64,256]{1,0:T(8,128)(2,1)S(1)}, u32[]{:S(2)}, u32[]{:S(2)}) collective-permute-start(bf16[64,256]{1,0:T(8,128)(2,1)S(1)} %broadcast_select_fusion.3), channel_id=1, source_target_pairs={{0,1},{1,0},{2,3},{3,2},{4,5},{5,4},{6,7},{7,6},{8,9},{9,8},{10,11... | collective-permute-start | bytes 98312 | tf_op jit(solution)/shard_map/ppermute | solution.py:12
  308.7 6.1 %collective-permute-start.13 = (f32[128,256]{1,0:T(8,128)S(1)}, f32[128,256]{1,0:T(8,128)S(1)}, u32[]{:S(2)}, u32[]{:S(2)}) collective-permute-start(f32[128,256]{1,0:T(8,128)S(1)} %slice_select_fusion), channel_id=1, source_target_pairs={{0,1},{1,0},{2,3},{3,2},{4,5},{5,4},{6,7},{7,6},{8,9},{9,8},{10,11... | collective-permute-start | bytes 393224 | tf_op jit(solution)/shard_map/ppermute | solution.py:12
  (11 other events, 44.0 us)
Sparse Core Ops, SparseCore 0:
  147.0 125.8 reduce-scatter.1
